TPU v7x, 128 devices: a whole 4x4x4 slice. The times are simulated.
128 devices in a mesh: dp: 16 (over y, x), mp: 8 (over z, core).
Axes of the slice: x: 4, y: 4, z: 4, core: 2. Of those that a mesh axis runs over, the one named last changes fastest.
Arguments:
- tokens: bfloat16 [8192, 4096], P('dp'), may hold values from -6 to 6
- cache: bfloat16 [384, 128, 896], P('dp'), may hold values from -220 to 220
- nb_row: int32 [128, 2], P('dp'), may hold values from 0 to 23
- nb_owner: int32 [128, 2], P('dp'), may hold values from 0 to 15, all different within a row; in each aligned block of 8 rows (0 to 7, 8 to 15, ...) at most 3 rows name the same one
- nb_len: int32 [128, 2], P('dp'), may hold values from 32 to 128, as said below
- w_query: bfloat16 [4096, 4096], P('dp', 'mp'), may hold values from -0.09375 to 0.09375
- w_key: bfloat16 [896, 4096], P('dp', 'mp'), may hold values from -0.1875 to 0.1875
- w_value: bfloat16 [896, 4096], P('dp', 'mp'), may hold values from -0.1875 to 0.1875
- w_out: bfloat16 [4096, 4096], P('mp', 'dp'), may hold values from -0.09375 to 0.09375
- grad_out: bfloat16 [8192, 4096], P('dp'), may hold values from -6 to 6
Outputs:
- mixed: bfloat16 [8192, 4096], P('dp', 'mp')
- grad_tokens: bfloat16 [8192, 4096], P('dp', 'mp')
- grad_query: float32 [4096, 4096], P('dp', 'mp')
- grad_key: float32 [896, 4096], P('dp', 'mp')
- grad_value: float32 [896, 4096], P('dp', 'mp')
- grad_wout: float32 [4096, 4096], P('mp', 'dp')
Inputs may be any that keep to these rules, and one draw needn't show every extreme that they name: `nb_owner`: among the 8 stretches of one index of dp no shard is named more than 3 times, a bound that some block reaches; the 2 neighbours of a stretch lie on different shards. `nb_len`: the first neighbour of every stretch has all 128 tokens.
All inputs are finite; a program needn't handle non-finite values.
Results may differ from a plain program's by a relative error of at most 0.014.
The roundings to bfloat16 on the way count: a program that leaves them out, or rounds other values in their place, can miss the bound.
Values may be sent and summed in bfloat16 or wider, within the bound.
No kernel may reach another device: no remote copies, remote signals or barrier semaphores. Data moves between devices by JAX's collectives and lax.ppermute only.
A program may use at most 128 MiB of HBM per device.

v0:
```python
import jax
import jax.numpy as jnp
from jax import lax
from jax.sharding import PartitionSpec as P

HD = 128
CL = 64
KN = 2
CAP = 3


def on_device(tokens, cache, nb_row, nb_owner, nb_len, w_query, w_key, w_value, w_out, grad_out):
    dp_count = lax.axis_size("dp")
    mp_count = lax.axis_size("mp")
    mp_place = lax.axis_index("mp")
    tok_rows, width = tokens.shape
    head_span = w_query.shape[1]
    heads_here = head_span // HD
    stretch_count = nb_row.shape[0]
    request_count = stretch_count * KN
    cache_rows, block_len, enc_width = cache.shape
    width_share = width // mp_count
    score_scale = HD ** (-0.5)
    wide_tokens = tokens.astype(jnp.float32)
    inv_rms = lax.rsqrt(jnp.mean(wide_tokens * wide_tokens, axis=1, keepdims=True) + 1e-06)
    normed_wide = wide_tokens * inv_rms
    normed = normed_wide.astype(jnp.bfloat16)
    query_full = lax.all_gather(w_query, "dp", axis=0, tiled=True)
    output_full = lax.all_gather(w_out, "dp", axis=1, tiled=True)
    queries = jnp.dot(normed, query_full, preferred_element_type=jnp.float32).astype(jnp.bfloat16)
    owners = nb_owner.reshape(-1)
    wanted = nb_row.reshape(-1)
    req_order = jnp.arange(request_count)
    earlier = (owners[:, None] == owners[None, :]) & (req_order[None, :] < req_order[:, None])
    rank_seen = jnp.sum(earlier.astype(jnp.int32), axis=1)
    slot_of = owners * CAP + rank_seen
    slot_hits = (slot_of[:, None] == jnp.arange(dp_count * CAP)[None, :]).astype(jnp.int32)
    asked_ids = (jnp.sum(slot_hits * (wanted[:, None] + 1), axis=0) - 1).reshape(dp_count, CAP)
    picked_rows = jnp.clip(
        lax.all_to_all(asked_ids, "dp", split_axis=0, concat_axis=0, tiled=True), 0, cache_rows - 1
    )
    picked = jnp.take(cache, picked_rows, axis=0)
    arrived = lax.all_to_all(picked, "dp", split_axis=0, concat_axis=0, tiled=True)
    arrived = arrived.reshape(dp_count * CAP, arrived.shape[2], enc_width)
    blocks = jnp.take(arrived, slot_of, axis=0)
    flat_blocks = blocks.reshape(request_count * block_len, enc_width)
    key_sum = jnp.dot(
        flat_blocks,
        lax.all_gather(w_key, "dp", axis=0, tiled=True),
        preferred_element_type=jnp.float32,
    )
    value_sum = jnp.dot(
        flat_blocks,
        lax.all_gather(w_value, "dp", axis=0, tiled=True),
        preferred_element_type=jnp.float32,
    )
    keys = key_sum.astype(jnp.bfloat16).reshape(stretch_count, KN * block_len, heads_here, HD)
    values = value_sum.astype(jnp.bfloat16).reshape(stretch_count, KN * block_len, heads_here, HD)
    positions = jnp.arange(block_len)
    key_valid = (positions[None, None, :] < nb_len[:, :, None]).reshape(
        stretch_count, KN * block_len
    )
    query_blocks = queries.reshape(stretch_count, CL, heads_here, HD)
    scores = (
        jnp.einsum("cqhd,ckhd->chqk", query_blocks, keys, preferred_element_type=jnp.float32)
        * score_scale
    )
    scores = jnp.where(key_valid[:, None, None, :], scores, -1e30)
    row_top = jnp.max(scores, axis=3, keepdims=True)
    weights_exp = jnp.exp(scores - row_top)
    prob_wide = weights_exp / jnp.sum(weights_exp, axis=3, keepdims=True)
    prob = prob_wide.astype(jnp.bfloat16)
    attended = jnp.einsum(
        "chqk,ckhd->cqhd", prob, values, preferred_element_type=jnp.float32
    ).astype(jnp.bfloat16)
    attended = attended.reshape(tok_rows, head_span)
    partial_out = jnp.dot(attended, output_full, preferred_element_type=jnp.float32)
    summed_out = lax.psum_scatter(
        partial_out.astype(jnp.bfloat16), "mp", scatter_dimension=1, tiled=True
    ).astype(jnp.float32)
    token_cols = lax.dynamic_slice_in_dim(wide_tokens, mp_place * width_share, width_share, 1)
    mixed = (token_cols + summed_out).astype(jnp.bfloat16)
    grad_attn = jnp.einsum(
        "td,sd->ts", grad_out, output_full, preferred_element_type=jnp.float32
    ).astype(jnp.bfloat16)
    grad_wout_part = jnp.einsum("ts,td->sd", attended, grad_out, preferred_element_type=jnp.float32)
    grad_blocks = grad_attn.reshape(stretch_count, CL, heads_here, HD)
    grad_prob = jnp.einsum(
        "cqhd,ckhd->chqk", grad_blocks, values, preferred_element_type=jnp.float32
    )
    grad_values = jnp.einsum(
        "chqk,cqhd->ckhd", prob, grad_blocks, preferred_element_type=jnp.float32
    ).astype(jnp.bfloat16)
    delta_rows = jnp.sum(prob_wide * grad_prob, axis=3, keepdims=True)
    grad_scores = (prob_wide * (grad_prob - delta_rows) * score_scale).astype(jnp.bfloat16)
    grad_queries = jnp.einsum(
        "chqk,ckhd->cqhd", grad_scores, keys, preferred_element_type=jnp.float32
    ).astype(jnp.bfloat16)
    grad_queries = grad_queries.reshape(tok_rows, head_span)
    grad_keys = jnp.einsum(
        "chqk,cqhd->ckhd", grad_scores, query_blocks, preferred_element_type=jnp.float32
    ).astype(jnp.bfloat16)
    grad_keys = grad_keys.reshape(request_count * block_len, head_span)
    grad_values = grad_values.reshape(request_count * block_len, head_span)
    grad_wq_part = jnp.einsum("td,ts->ds", normed, grad_queries, preferred_element_type=jnp.float32)
    grad_wk_part = jnp.einsum(
        "re,rs->es", flat_blocks, grad_keys, preferred_element_type=jnp.float32
    )
    grad_wv_part = jnp.einsum(
        "re,rs->es", flat_blocks, grad_values, preferred_element_type=jnp.float32
    )
    grad_query, grad_key, grad_value, grad_wout = (
        lax.psum_scatter(
            grad_wq_part.astype(jnp.bfloat16), "dp", scatter_dimension=0, tiled=True
        ).astype(jnp.float32),
        lax.psum_scatter(
            grad_wk_part.astype(jnp.bfloat16), "dp", scatter_dimension=0, tiled=True
        ).astype(jnp.float32),
        lax.psum_scatter(
            grad_wv_part.astype(jnp.bfloat16), "dp", scatter_dimension=0, tiled=True
        ).astype(jnp.float32),
        lax.psum_scatter(
            grad_wout_part.astype(jnp.bfloat16), "dp", scatter_dimension=1, tiled=True
        ).astype(jnp.float32),
    )
    grad_normed_part = jnp.einsum(
        "ts,ds->td", grad_queries, query_full, preferred_element_type=jnp.float32
    )
    out_cols = lax.dynamic_slice_in_dim(grad_out, mp_place * width_share, width_share, 1).astype(
        jnp.float32
    )
    grad_normed = lax.psum(grad_normed_part.astype(jnp.bfloat16), "mp").astype(jnp.float32)
    stat_rows = jnp.mean(grad_normed * normed_wide, axis=1, keepdims=True)
    grad_full = inv_rms * (grad_normed - normed_wide * stat_rows)
    grad_here = lax.dynamic_slice_in_dim(grad_full, mp_place * width_share, width_share, 1)
    grad_tokens = (out_cols + grad_here).astype(jnp.bfloat16)
    return (mixed, grad_tokens, grad_query, grad_key, grad_value, grad_wout)


def solution(mesh):
    return jax.shard_map(
        on_device,
        mesh=mesh,
        in_specs=(
            P("dp", None),
            P("dp", None, None),
            P("dp", None),
            P("dp", None),
            P("dp", None),
            P("dp", "mp"),
            P("dp", "mp"),
            P("dp", "mp"),
            P("mp", "dp"),
            P("dp", None),
        ),
        out_specs=(
            P("dp", "mp"),
            P("dp", "mp"),
            P("dp", "mp"),
            P("dp", "mp"),
            P("dp", "mp"),
            P("mp", "dp"),
        ),
        check_vma=False,
    )
```

profile of v0, /device:TPU:0, one launch (start us, length us, event | category | flops | bytes accessed | tf_op | source)
XLA Modules:
  0.0 782.3 jit_solution(9086871764430105319)
XLA Ops:
  7.2 0.7 all-gather.3.cloned.1.call-update
  7.9 0.7 broadcast_add_fusion
  8.7 0.8 copy.90
  9.6 0.2 convert_reduce_fusion
  10.0 14.5 %all_to_all.11 = s32[16,1,3]{2,1,0:T(1,128)S(1)} all-to-all(s32[16,1,3]{2,1,0:T(1,128)S(1)} %bitcast.84), channel_id=1, replica_groups=mesh['dp'=16,'mp'=8] {'dp'}, dimensions={0} | all-to-all | bytes 384 | tf_op jit(solution)/shard_map/all_to_all | solution.py:40
  24.9 9.8 %gather_fusion = bf16[48,128,896]{2,1,0:T(8,128)(2,1)} fusion(bf16[24,128,896]{2,1,0:T(8,128)(2,1)} %param.11, s32[1024]{0:T(1024)S(1)} %pad_clamp_fusion.1), kind=kCustom, calls=%fused_computation | custom fusion | bytes 22020288 | tf_op jit(solution)/shard_map/jit(_take)/gather | solution.py:42
  34.7 10.0 %broadcast_select_fusion = bf16[16,3,128,896]{3,2,1,0:T(8,128)(2,1)} fusion(bf16[16,3,128,896]{3,2,1,0:T(8,128)(2,1)} %bitcast.73, pred[16,3]{1,0:T(8,128)(4,1)S(1)} %copy.94), kind=kLoop, calls=%fused_computation.4 | loop fusion | flops 5505024 | bytes 22020144 | tf_op jit(solution)/shard_map/jit(_take)/select_n | solution.py:42
  44.7 5.0 all-to-all-start.1
  49.7 0.7 all-gather.5.cloned.1.call-update
  50.7 191.9 %all_gather.12 = bf16[896,512]{1,0:T(8,128)(2,1)S(1)} all-gather(bf16[56,512]{1,0:T(8,128)(2,1)S(1)} %copy-done.7), channel_id=1, replica_groups=mesh['dp'=16,'mp'=8] {'dp'}, dimensions={0}, use_global_device_ids=true | all-gather | bytes 974848 | tf_op jit(solution)/shard_map/all_gather | solution.py:54
  242.7 27.2 %all_gather.14 = bf16[896,512]{1,0:T(8,128)(2,1)} all-gather(bf16[56,512]{1,0:T(8,128)(2,1)S(1)} %copy-done.8), channel_id=1, replica_groups=mesh['dp'=16,'mp'=8] {'dp'}, dimensions={0}, use_global_device_ids=true | all-gather | bytes 974848 | tf_op jit(solution)/shard_map/all_gather | solution.py:49
  269.9 3.1 multiply_reduce_fusion.1
  273.1 5.8 fusion.29
  278.9 0.1 reshape.230
  279.1 5.8 convolution_convert_fusion.8
  284.9 0.1 reshape.233
  285.1 7.0 gather_fusion.1
  292.1 4.4 broadcast_select_fusion.1
  296.5 0.9 bitcast_select_fusion
  297.4 1.8 copy-done.6
  299.3 3.8 convolution_convert_fusion.5
  303.1 2.5 reshape.229
  305.6 6.0 convolution_convert_fusion.4
  311.6 4.1 reshape.231
  315.7 2.4 fusion.15
  318.2 2.1 fusion.70
  320.3 2.2 fusion.9
  322.5 16.6 %convert_bitcast_fusion.1 = bf16[8,256,4,128]{1,3,2,0:T(8,128)(2,1)} fusion(f32[8,4,64,256]{3,2,1,0:T(8,128)} %fusion.9, bf16[8,64,4,128]{3,2,1,0:T(4,128)(2,1)S(1)} %reshape.230, f32[8,4,64,256]{3,2,1,0:T(8,128)} %get-tuple-element.11, f32[8,4,64]{2,1,0:T(4,128)S(1)} %get-tuple-element.10), kind=kOutput, calls=%fused_computation.17 | convolution fusion | flops 138938624 | bytes 6823936 | tf_op jit(solution)/shard_map/chqk,cqhd->ckhd/dot_general | solution.py:100
  339.0 2.8 copy.106
  341.8 0.7 copy.112
  342.5 1.3 copy-done.4
  343.8 3.0 convolution_convert_fusion.7
  346.9 0.3 reduce-scatter.18.cloned.1.call-start
  347.2 7.0 convert_bitcast_fusion
  354.2 2.8 copy.108
  357.0 0.7 copy.113
  357.7 1.3 copy-done.5
  359.0 3.0 convolution_convert_fusion.6
  362.1 15.3 %fusion.35 = bf16[8,64,4,128]{3,1,2,0:T(8,128)(2,1)S(1)} fusion(bf16[8,256,4,128]{3,2,1,0:T(4,128)(2,1)} %reshape.231, f32[8,4,64,256]{3,2,1,0:T(8,128)} %fusion.9, f32[8,4,64,256]{3,2,1,0:T(8,128)} %get-tuple-element.11, f32[8,4,64]{2,1,0:T(4,128)S(1)} %get-tuple-element.10), kind=kOutput, calls=%fused_computation.42 | convolution fusion | flops 138152192 | bytes 6823936 | tf_op jit(solution)/shard_map/chqk,ckhd->cqhd/dot_general | solution.py:96
  377.4 0.4 copy.104
  377.9 6.6 convolution_convert_fusion.2
  384.5 0.3 reduce-scatter.12.cloned.1.call-start
  384.8 6.6 convolution_convert_fusion.1
  391.5 5.3 fusion.32
  396.7 0.4 copy.100
  397.2 6.5 convolution_convert_fusion
  403.7 0.3 reduce-scatter.10.cloned.1.call-start
  404.1 6.6 convolution_convert_fusion.3
  410.7 6.5 convert_element_type.97
  417.2 2.3 reduce-scatter.16.cloned.1.call-done
  419.5 1.5 convert_element_type.122
  421.0 74.8 %reduce-scatter.18.cloned.1.call-done = bf16[56,512]{1,0:T(8,128)(2,1)} async-done(((bf16[896,512]{1,0:T(8,128)(2,1)}), bf16[56,512]{1,0:T(8,128)(2,1)}) %reduce-scatter.18.cloned.1.call-update) | async-done | bytes 57360
  495.8 1.5 convert_element_type.126
  497.3 72.8 %all-reduce.4.cloned.1.call-done = bf16[512,4096]{1,0:T(8,128)(2,1)} async-done(((bf16[512,4096]{1,0:T(8,128)(2,1)}), bf16[512,4096]{1,0:T(8,128)(2,1)}) %all-reduce.4.cloned.1.call-update) | async-done | bytes 4194320 | tf_op jit(solution)/shard_map/psum | solution.py:132
  570.1 3.4 convert_element_type.115
  573.6 1.3 copy-done.2
  574.8 4.6 multiply_reduce_fusion
  579.5 2.5 fusion.42
  582.0 69.7 %reduce-scatter.12.cloned.1.call-done = bf16[256,512]{1,0:T(8,128)(2,1)} async-done(((bf16[4096,512]{1,0:T(8,128)(2,1)}), bf16[256,512]{1,0:T(8,128)(2,1)}) %reduce-scatter.12.cloned.1.call-update) | async-done | bytes 262160 | tf_op jit(solution)/shard_map/reduce_scatter | solution.py:113
  651.7 1.8 convert_element_type.118
  653.5 79.3 %reduce-scatter.14.cloned.1.call-done = bf16[512,256]{1,0:T(8,128)(2,1)} async-done(((bf16[512,4096]{1,0:T(8,128)(2,1)}), bf16[512,256]{1,0:T(8,128)(2,1)}) %reduce-scatter.14.cloned.1.call-update) | async-done | bytes 262160 | tf_op jit(solution)/shard_map/reduce_scatter | solution.py:122
  732.8 1.8 convert_element_type.128
  734.6 38.1 %reduce-scatter.10.cloned.1.call-done = bf16[512,512]{1,0:T(8,128)(2,1)} async-done(((bf16[512,4096]{1,0:T(8,128)(2,1)}), bf16[512,512]{1,0:T(8,128)(2,1)}) %reduce-scatter.10.cloned.1.call-update) | async-done | bytes 524304 | tf_op jit(solution)/shard_map/reduce_scatter | solution.py:78
  772.7 2.3 add_convert_fusion
  (57 shorter events, 1.5 us)
Async XLA Ops:
  7.2 265.9 %all-gather.3.cloned.1.call-start = ((), (), s32[]{:S(2)}) async-start(), calls=%async_computation.7 | async-start | bytes 4456448 | tf_op jit(solution)/shard_map/all_gather | solution.py:28
  44.7 5.8 copy-start.9
  44.7 6.0 copy-start.7
  44.7 198.0 %copy-start.8 = (bf16[56,512]{1,0:T(8,128)(2,1)S(1)}, bf16[56,512]{1,0:T(8,128)(2,1)}, u32[]{:S(2)}) copy-start(bf16[56,512]{1,0:T(8,128)(2,1)} %param.16) | copy-start | bytes 172036
  44.7 240.4 %all-to-all-start.1 = ((bf16[16,3,128,896]{3,2,1,0:T(8,128)(2,1)}), bf16[16,3,128,896]{3,2,1,0:T(8,128)(2,1)}, u32[]{:S(2)}, u32[]{:S(2)}) async-start(bf16[16,3,128,896]{3,2,1,0:T(8,128)(2,1)} %broadcast_select_fusion), calls=%async_computation.1 | async-start | bytes 22020096 | tf_op jit(solution)/shard_map/all_to_all | solution.py:43
  49.7 229.4 %all-gather.5.cloned.1.call-start = ((), (), s32[]{:S(2)}) async-start(), calls=%async_computation.8 | async-start | bytes 4456448 | tf_op jit(solution)/shard_map/all_gather | solution.py:29
  50.4 369.0 %reduce-scatter.16.cloned.1.call-start = ((), (), s32[]{:S(2)}) async-start(), calls=%async_computation.13 | async-start | bytes 974848
  269.9 3.1 copy-start.10
  292.1 4.4 copy-start.1
  297.4 1.8 copy-start.6
  318.2 2.1 copy-start.3
  341.8 2.0 copy-start.4
  346.9 148.9 %reduce-scatter.18.cloned.1.call-start = ((), (), s32[]{:S(2)}) async-start(), calls=%async_computation.14 | async-start | bytes 974848
  357.0 2.0 copy-start.5
  362.1 208.0 %all-reduce.4.cloned.1.call-start = ((), (), s32[]{:S(2)}) async-start(), calls=%async_computation.10 | async-start | bytes 8388608 | tf_op jit(solution)/shard_map/psum | solution.py:132
  384.5 267.2 %reduce-scatter.12.cloned.1.call-start = ((), (), s32[]{:S(2)}) async-start(), calls=%async_computation.11 | async-start | bytes 4456448 | tf_op jit(solution)/shard_map/reduce_scatter | solution.py:113
  391.4 341.3 %reduce-scatter.14.cloned.1.call-start = ((), (), s32[]{:S(2)}) async-start(), calls=%async_computation.12 | async-start | bytes 4456448 | tf_op jit(solution)/shard_map/reduce_scatter | solution.py:122
  403.7 368.9 %reduce-scatter.10.cloned.1.call-start = ((), (), s32[]{:S(2)}) async-start(), calls=%async_computation.9 | async-start | bytes 4718592 | tf_op jit(solution)/shard_map/reduce_scatter | solution.py:78
  570.1 3.4 copy-start
  570.1 4.7 copy-start.2
Sparse Core Ops, SparseCore 0:
  10.1 158.5 all-gather.2
  170.8 90.4 all-gather.4
  347.0 72.4 reduce-scatter.15
  422.5 73.2 reduce-scatter.17
  498.0 72.0 all-reduce.3
  573.3 78.3 reduce-scatter.11
  655.0 77.7 reduce-scatter.13
  735.2 37.4 reduce-scatter.9
where the time goes:
time: 787 us; the launch traced here: 782 us
  waiting for transfers between devices  339 us (43%)
  blocking collectives  234 us (30%)
  matrix products  103 us (13%)
  other arithmetic  47.6 us (6%)
  local copies, waits for them, and re-layouts  39 us (5%)
  between operations  14.9 us (2%)
    all_gather x1, blocking collectives, on_device(): lax.all_gather(w_value, 'dp', axis=0, tiled=True)  192 us
    reduce_scatter x1, waiting for transfers between devices, on_device(): lax.psum_scatter(grad_wout_part.astype(jnp.bfloat16), 'dp', scatter_dimen...  79.3 us
    unnamed x10, waiting for transfers between devices  78.6 us
    psum x1, waiting for transfers between devices, on_device(): lax.psum(grad_normed_part.astype(jnp.bfloat16), 'mp').astype(jnp.float32)  72.8 us
    reduce_scatter x1, waiting for transfers between devices, on_device(): lax.psum_scatter(grad_wq_part.astype(jnp.bfloat16), 'dp', scatter_dimensi...  69.7 us
    reduce_scatter x1, waiting for transfers between devices, on_device(): lax.psum_scatter(partial_out.astype(jnp.bfloat16), 'mp', scatter_dimensio...  38.1 us
    all_gather x1, blocking collectives, on_device(): lax.all_gather(w_key, 'dp', axis=0, tiled=True)  27.2 us
    dot_general x1, matrix products, on_device(): jnp.einsum('chqk,cqhd->ckhd', grad_scores, query_blocks, preferred_elemen...  16.6 us
  transfers between devices with their start and end apart: 9, of which 6 were waited for; matrix products, arithmetic and copies ran while one was open for 16% of the time, Pallas kernels for 0%

commit v1 on v0

--- a/solution.py
+++ b/solution.py
@@ -129,7 +129,9 @@
     out_cols = lax.dynamic_slice_in_dim(grad_out, mp_place * width_share, width_share, 1).astype(
         jnp.float32
     )
-    grad_normed = lax.psum(grad_normed_part.astype(jnp.bfloat16), "mp").astype(jnp.float32)
+    grad_normed = jnp.sum(
+        lax.all_gather(grad_normed_part.astype(jnp.bfloat16), "mp"), axis=0
+    ).astype(jnp.float32)
     stat_rows = jnp.mean(grad_normed * normed_wide, axis=1, keepdims=True)
     grad_full = inv_rms * (grad_normed - normed_wide * stat_rows)
     grad_here = lax.dynamic_slice_in_dim(grad_full, mp_place * width_share, width_share, 1)

time: 787 us -> 884 us (1.12)
  waiting for transfers between devices: 339 us -> 429 us
  other arithmetic: 47.6 us -> 61.4 us
    all_gather x1, blocking collectives: 192 us -> 27.2 us  [on_device(): lax.all_gather(w_value, 'dp', axis=0, tiled=True)]
    all_gather x1, blocking collectives: 27.2 us -> 192 us  [on_device(): lax.all_gather(w_key, 'dp', axis=0, tiled=True)]
    all_gather x0 -> x1, waiting for transfers between devices: none -> 154 us  [on_device(): lax.all_gather(grad_normed_part.astype(jnp.bfloat16), 'mp')]
    psum x1 -> x0, waiting for transfers between devices: 72.8 us -> none  [on_device(): lax.psum(grad_normed_part.astype(jnp.bfloat16), 'mp').astype(jnp.float32)]
    reduce_sum x0 -> x1, other arithmetic: none -> 14.2 us  [on_device(): jnp.sum(lax.all_gather(grad_normed_part.astype(jnp.bfloat16), 'mp'), axis=0)]
    reduce_scatter x1, waiting for transfers between devices: 69.7 us -> 79.2 us  [on_device(): lax.psum_scatter(grad_wq_part.astype(jnp.bfloat16), 'dp', scatter_dimensi...]
  transfers between devices with their start and end apart: 9 -> 9, of which waited for: 6 -> 6; matrix products, arithmetic and copies ran while one was open for 16% -> 13% of each run, Pallas kernels for 0% -> 0%
where the time goes in v1:
time: 884 us; the launch traced here: 879 us
  waiting for transfers between devices  429 us (49%)
  blocking collectives  234 us (26%)
  matrix products  97.3 us (11%)
  other arithmetic  61.4 us (7%)
  local copies, waits for them, and re-layouts  36.1 us (4%)
  between operations  14.9 us (2%)
    all_gather x1, blocking collectives, on_device(): lax.all_gather(w_key, 'dp', axis=0, tiled=True)  192 us
    all_gather x1, waiting for transfers between devices, on_device(): lax.all_gather(grad_normed_part.astype(jnp.bfloat16), 'mp')  154 us
    reduce_scatter x1, waiting for transfers between devices, on_device(): lax.psum_scatter(grad_wout_part.astype(jnp.bfloat16), 'dp', scatter_dimen...  79.5 us
    reduce_scatter x1, waiting for transfers between devices, on_device(): lax.psum_scatter(grad_wq_part.astype(jnp.bfloat16), 'dp', scatter_dimensi...  79.2 us
    unnamed x10, waiting for transfers between devices  78.6 us
    reduce_scatter x1, waiting for transfers between devices, on_device(): lax.psum_scatter(partial_out.astype(jnp.bfloat16), 'mp', scatter_dimensio...  38 us
    all_gather x1, blocking collectives, on_device(): lax.all_gather(w_value, 'dp', axis=0, tiled=True)  27.2 us
  transfers between devices with their start and end apart: 9, of which 6 were waited for; matrix products, arithmetic and copies ran while one was open for 13% of the time, Pallas kernels for 0%

profile of v1, /device:TPU:0, one launch (start us, length us, event | category | flops | bytes accessed | tf_op | source)
XLA Modules:
  0.0 878.7 jit_solution(9485151459332659931)
XLA Ops:
  7.2 0.7 all-gather.5.cloned.1.call-update
  7.9 0.7 broadcast_add_fusion
  8.7 0.8 copy.90
  9.6 0.2 convert_reduce_fusion
  10.0 14.5 %all_to_all.11 = s32[16,1,3]{2,1,0:T(1,128)S(1)} all-to-all(s32[16,1,3]{2,1,0:T(1,128)S(1)} %bitcast.86), channel_id=1, replica_groups=mesh['dp'=16,'mp'=8] {'dp'}, dimensions={0} | all-to-all | bytes 384 | tf_op jit(solution)/shard_map/all_to_all | solution.py:40
  24.9 9.8 %gather_fusion = bf16[48,128,896]{2,1,0:T(8,128)(2,1)} fusion(bf16[24,128,896]{2,1,0:T(8,128)(2,1)} %param.11, s32[1024]{0:T(1024)S(1)} %pad_clamp_fusion.1), kind=kCustom, calls=%fused_computation | custom fusion | bytes 22020288 | tf_op jit(solution)/shard_map/jit(_take)/gather | solution.py:42
  34.7 10.0 %broadcast_select_fusion = bf16[16,3,128,896]{3,2,1,0:T(8,128)(2,1)} fusion(bf16[16,3,128,896]{3,2,1,0:T(8,128)(2,1)} %bitcast.74, pred[16,3]{1,0:T(8,128)(4,1)S(1)} %copy.94), kind=kLoop, calls=%fused_computation.4 | loop fusion | flops 5505024 | bytes 22020144 | tf_op jit(solution)/shard_map/jit(_take)/select_n | solution.py:42
  44.7 5.0 all-to-all-start.1
  49.7 0.7 all-gather.7.cloned.1.call-update
  50.7 191.9 %all_gather.20 = bf16[896,512]{1,0:T(8,128)(2,1)S(1)} all-gather(bf16[56,512]{1,0:T(8,128)(2,1)S(1)} %copy-done.8), channel_id=1, replica_groups=mesh['dp'=16,'mp'=8] {'dp'}, dimensions={0}, use_global_device_ids=true | all-gather | bytes 974848 | tf_op jit(solution)/shard_map/all_gather | solution.py:49
  242.6 27.2 %all_gather.18 = bf16[896,512]{1,0:T(8,128)(2,1)} all-gather(bf16[56,512]{1,0:T(8,128)(2,1)S(1)} %copy-done.9), channel_id=1, replica_groups=mesh['dp'=16,'mp'=8] {'dp'}, dimensions={0}, use_global_device_ids=true | all-gather | bytes 974848 | tf_op jit(solution)/shard_map/all_gather | solution.py:54
  269.9 3.1 multiply_reduce_fusion.1
  273.1 5.8 fusion.29
  278.9 0.1 reshape.230
  279.1 5.8 convolution_convert_fusion.8
  285.0 7.0 gather_fusion.1
  292.1 4.4 broadcast_select_fusion.1
  296.5 0.9 bitcast_select_fusion
  297.4 3.7 convolution_convert_fusion.4
  301.1 2.4 convolution_convert_fusion.5
  303.5 2.1 reshape.229
  305.6 2.7 reshape.231
  308.4 0.8 fusion.15
  309.2 0.7 copy-done.3
  310.0 2.1 fusion.9
  312.1 1.8 fusion.70
  313.9 16.6 %convert_bitcast_fusion.1 = bf16[8,256,4,128]{1,3,2,0:T(8,128)(2,1)} fusion(f32[8,4,64,256]{3,2,1,0:T(8,128)} %fusion.9, bf16[8,64,4,128]{3,2,1,0:T(4,128)(2,1)S(1)} %reshape.230, f32[8,4,64,256]{3,2,1,0:T(8,128)} %get-tuple-element.11, f32[8,4,64]{2,1,0:T(4,128)S(1)} %get-tuple-element.10), kind=kOutput, calls=%fused_computation.17 | convolution fusion | flops 138938624 | bytes 6823936 | tf_op jit(solution)/shard_map/chqk,cqhd->ckhd/dot_general | solution.py:100
  330.5 2.8 copy.106
  333.3 0.7 copy.112
  334.0 1.3 copy-done.5
  335.3 3.1 convolution_convert_fusion.7
  338.4 0.3 reduce-scatter.18.cloned.1.call-start
  338.6 7.0 convert_bitcast_fusion
  345.7 2.8 copy.108
  348.5 0.7 copy.113
  349.2 1.3 copy-done.6
  350.5 3.1 convolution_convert_fusion.6
  353.6 5.9 fusion.32
  359.5 0.4 copy.100
  359.9 6.5 convolution_convert_fusion
  366.4 0.3 reduce-scatter.12.cloned.1.call-start
  366.7 14.7 %fusion.35 = bf16[8,64,4,128]{3,1,2,0:T(8,128)(2,1)S(1)} fusion(bf16[8,256,4,128]{3,2,1,0:T(4,128)(2,1)S(1)} %reshape.231, f32[8,4,64,256]{3,2,1,0:T(8,128)} %fusion.9, f32[8,4,64,256]{3,2,1,0:T(8,128)} %get-tuple-element.11, f32[8,4,64]{2,1,0:T(4,128)S(1)} %get-tuple-element.10), kind=kOutput, calls=%fused_computation.42 | convolution fusion | flops 138152192 | bytes 6823936 | tf_op jit(solution)/shard_map/chqk,ckhd->cqhd/dot_general | solution.py:96
  381.5 0.4 copy.104
  381.9 6.6 convolution_convert_fusion.1
  388.6 6.5 convolution_convert_fusion.3
  395.1 0.3 all-gather.9.cloned.1.call-start
  395.5 6.6 convolution_convert_fusion.2
  402.1 6.5 convert_element_type.99
  408.6 2.3 reduce-scatter.16.cloned.1.call-done
  410.9 1.5 convert_element_type.124
  412.4 74.9 %reduce-scatter.18.cloned.1.call-done = bf16[56,512]{1,0:T(8,128)(2,1)} async-done(((bf16[896,512]{1,0:T(8,128)(2,1)}), bf16[56,512]{1,0:T(8,128)(2,1)}) %reduce-scatter.18.cloned.1.call-update) | async-done | bytes 57360
  487.2 1.5 convert_element_type.128
  488.7 79.5 %reduce-scatter.14.cloned.1.call-done = bf16[512,256]{1,0:T(8,128)(2,1)} async-done(((bf16[512,4096]{1,0:T(8,128)(2,1)}), bf16[512,256]{1,0:T(8,128)(2,1)}) %reduce-scatter.14.cloned.1.call-update) | async-done | bytes 262160 | tf_op jit(solution)/shard_map/reduce_scatter | solution.py:122
  568.2 1.8 convert_element_type.130
  570.0 79.2 %reduce-scatter.12.cloned.1.call-done = bf16[256,512]{1,0:T(8,128)(2,1)} async-done(((bf16[4096,512]{1,0:T(8,128)(2,1)}), bf16[256,512]{1,0:T(8,128)(2,1)}) %reduce-scatter.12.cloned.1.call-update) | async-done | bytes 262160 | tf_op jit(solution)/shard_map/reduce_scatter | solution.py:113
  649.1 1.8 convert_element_type.120
  650.9 38.0 %reduce-scatter.10.cloned.1.call-done = bf16[512,512]{1,0:T(8,128)(2,1)} async-done(((bf16[512,4096]{1,0:T(8,128)(2,1)}), bf16[512,512]{1,0:T(8,128)(2,1)}) %reduce-scatter.10.cloned.1.call-update) | async-done | bytes 524304 | tf_op jit(solution)/shard_map/reduce_scatter | solution.py:78
  689.0 2.3 add_convert_fusion
  691.3 154.0 %all-gather.9.cloned.1.call-done = bf16[4096,4096]{1,0:T(8,128)(2,1)} async-done(((bf16[512,4096]{1,0:T(8,128)(2,1)}), bf16[4096,4096]{1,0:T(8,128)(2,1)}) %all-gather.9.cloned.1.call-update) | async-done | bytes 33554448 | tf_op jit(solution)/shard_map/all_gather | solution.py:133
  845.4 14.2 %reduce_sum.74 = bf16[512,4096]{1,0:T(8,128)(2,1)} reduce(bf16[8,512,4096]{2,1,0:T(8,128)(2,1)} %bitcast.75, bf16[]{:T(256)} %constant.63.clone.1), dimensions={0}, to_apply=%region_7.8 | reduce | flops 14680064 | bytes 37748736 | tf_op jit(solution)/shard_map/reduce_sum | solution.py:132
  859.5 3.4 convert_element_type.117
  863.0 1.3 copy-done.1
  864.2 4.6 multiply_reduce_fusion
  868.9 2.5 fusion.42
  (60 shorter events, 1.7 us)
Async XLA Ops:
  7.2 265.9 %all-gather.5.cloned.1.call-start = ((), (), s32[]{:S(2)}) async-start(), calls=%async_computation.7 | async-start | bytes 4456448 | tf_op jit(solution)/shard_map/all_gather | solution.py:28
  44.7 5.8 copy-start.10
  44.7 6.0 copy-start.8
  44.7 197.9 %copy-start.9 = (bf16[56,512]{1,0:T(8,128)(2,1)S(1)}, bf16[56,512]{1,0:T(8,128)(2,1)}, u32[]{:S(2)}) copy-start(bf16[56,512]{1,0:T(8,128)(2,1)} %param.17) | copy-start | bytes 172036
  44.7 240.4 %all-to-all-start.1 = ((bf16[16,3,128,896]{3,2,1,0:T(8,128)(2,1)}), bf16[16,3,128,896]{3,2,1,0:T(8,128)(2,1)}, u32[]{:S(2)}, u32[]{:S(2)}) async-start(bf16[16,3,128,896]{3,2,1,0:T(8,128)(2,1)} %broadcast_select_fusion), calls=%async_computation.1 | async-start | bytes 22020096 | tf_op jit(solution)/shard_map/all_to_all | solution.py:43
  49.7 229.4 %all-gather.7.cloned.1.call-start = ((), (), s32[]{:S(2)}) async-start(), calls=%async_computation.8 | async-start | bytes 4456448 | tf_op jit(solution)/shard_map/all_gather | solution.py:29
  50.4 360.5 %reduce-scatter.16.cloned.1.call-start = ((), (), s32[]{:S(2)}) async-start(), calls=%async_computation.13 | async-start | bytes 974848
  269.9 3.1 copy-start.11
  292.1 4.4 copy-start.2
  297.4 3.7 copy-start.7
  308.4 1.6 copy-start.3
  310.0 2.2 copy-start.4
  333.3 2.0 copy-start.5
  338.4 148.8 %reduce-scatter.18.cloned.1.call-start = ((), (), s32[]{:S(2)}) async-start(), calls=%async_computation.14 | async-start | bytes 974848
  348.5 2.0 copy-start.6
  353.6 214.6 %reduce-scatter.14.cloned.1.call-start = ((), (), s32[]{:S(2)}) async-start(), calls=%async_computation.11 | async-start | bytes 4456448 | tf_op jit(solution)/shard_map/reduce_scatter | solution.py:122
  366.4 282.7 %reduce-scatter.12.cloned.1.call-start = ((), (), s32[]{:S(2)}) async-start(), calls=%async_computation.10 | async-start | bytes 4456448 | tf_op jit(solution)/shard_map/reduce_scatter | solution.py:113
  388.6 300.4 %reduce-scatter.10.cloned.1.call-start = ((), (), s32[]{:S(2)}) async-start(), calls=%async_computation.9 | async-start | bytes 4718592 | tf_op jit(solution)/shard_map/reduce_scatter | solution.py:78
  395.1 450.2 %all-gather.9.cloned.1.call-start = ((), (), s32[]{:S(2)}) async-start(), calls=%async_computation.12 | async-start | bytes 37748736 | tf_op jit(solution)/shard_map/all_gather | solution.py:133
  859.5 3.4 copy-start
  859.5 4.7 copy-start.1
Sparse Core Ops, SparseCore 0:
  10.1 158.5 all-gather.4
  170.8 90.3 all-gather.6
  338.5 72.3 reduce-scatter.15
  414.0 73.2 reduce-scatter.17
  490.4 77.7 reduce-scatter.13
  571.4 77.7 reduce-scatter.11
  651.5 37.4 reduce-scatter.9
  690.7 154.6 all-gather.8
